TPU v7x, 512 devices: a whole 4x4x16 slice. The times are simulated.
512 devices in a mesh: lon: 32 (over z_lo, y), lat: 16 (over z_hi, x, core).
Axes of the slice: x: 4, y: 4, z: 16 (z_hi: 2, z_lo: 8; z = z_hi * 8 + z_lo), core: 2. Of those that a mesh axis runs over, the one named last changes fastest.
Arguments:
- fields: bfloat16 [16, 64, 32, 4096], P('lat', None, None, 'lon'), may hold values from -40 to 40
- ocean_mask: int32 [16, 32, 4096], P('lat', None, 'lon'), may hold values 0 or 1
- norm_gain: float32 [64], replicated, may hold values from 0.5 to 1.5
- w_vert: bfloat16 [5, 8, 8, 8], replicated, may hold values from -1 to 1
- b_vert: float32 [64], replicated, may hold values from -3 to 3
- w_horiz: bfloat16 [5, 64, 5, 64], replicated, may hold values from -0.15625 to 0.15625
- b_horiz: float32 [64], replicated, may hold values from -3 to 3
Outputs:
- updated: bfloat16 [16, 64, 32, 4096], P('lat', None, None, 'lon')
All inputs are finite; a program needn't handle non-finite values. No bound on the sum of `ocean_mask` on one device may be relied on, other than what follows from the above.
Results may differ from a plain program's by a relative error of at most 0.0023.
Values may be sent and summed in bfloat16 or wider, within the bound.
A program may use at most 64 MiB of HBM per device.

v0:
```python
import jax
import jax.numpy as jnp
from jax import lax
from jax.sharding import PartitionSpec as P


def extended_2(shard, sides, width):
    for axis, dim in sides:
        devices, length = (lax.axis_size(axis), shard.shape[dim])
        up = [(i, (i + 1) % devices) for i in range(devices)]
        down = [(j, i) for i, j in up]
        last = lax.slice_in_dim(shard, length - width, length, axis=dim)
        leading = lax.slice_in_dim(shard, 0, width, axis=dim)
        before = lax.ppermute(last, axis, up)
        after = lax.ppermute(leading, axis, down)
        shard = jnp.concatenate([before, shard, after], axis=dim)
    return shard


def normalize(block, norm_gain):
    values = block.astype(jnp.float32)
    center = jnp.mean(values, axis=1, keepdims=True)
    spread = jnp.mean((values - center) ** 2, axis=1, keepdims=True)
    return ((values - center) * lax.rsqrt(spread + 1e-05) * norm_gain[None, :, None, None]).astype(
        jnp.bfloat16
    )


def vertical(taps, w_vert, b_vert):
    count_lev, channels, rows_lat, cols_lon = taps[0].shape
    groups, width_in, width_out = (w_vert.shape[1], w_vert.shape[2], w_vert.shape[3])
    summed = jnp.zeros((count_lev, groups, width_out, rows_lat, cols_lon), jnp.float32)
    for tap_index in range(len(taps)):
        grouped = taps[tap_index].reshape(count_lev, groups, width_in, rows_lat, cols_lon)
        summed = summed + jnp.einsum(
            "gio,ngiab->ngoab", w_vert[tap_index], grouped, preferred_element_type=jnp.float32
        )
    summed = summed.reshape(count_lev, channels, rows_lat, cols_lon) + b_vert[None, :, None, None]
    return jax.nn.gelu(summed).astype(jnp.bfloat16)


def shifted(block, axis, offset):
    devices = lax.axis_size(axis)
    pairs = [(i, i - offset) for i in range(devices) if 0 <= i - offset < devices]
    return lax.ppermute(block, axis, pairs)


def lon_halo(block, width):
    devices = lax.axis_size("lon")
    length = block.shape[-1]
    up = [(i, (i + 1) % devices) for i in range(devices)]
    down = [(j, i) for i, j in up]
    before = lax.ppermute(block[..., length - width :], "lon", up)
    after = lax.ppermute(block[..., :width], "lon", down)
    return (before, after)


def local(fields, ocean_mask, norm_gain, w_vert, b_vert, w_horiz, b_horiz):
    reach = w_vert.shape[0] // 2
    lat = ("lat_hi", "lat_lo")
    field_before, field_after = lon_halo(fields, reach)
    mask_before, mask_after = lon_halo(ocean_mask, reach)
    halo = jnp.concatenate([field_before, field_after], axis=3)
    halo_normed = normalize(halo, norm_gain)
    halo_taps = [
        halo_normed if tap == reach else shifted(halo_normed, lat, tap - reach)
        for tap in range(w_vert.shape[0])
    ]
    halo_mask = jnp.concatenate([mask_before, mask_after], axis=2)
    halo_masked = vertical(halo_taps, w_vert, b_vert) * halo_mask[:, None].astype(jnp.bfloat16)
    normed = normalize(fields, norm_gain)
    columns = lax.all_to_all(normed, "lat_lo", split_axis=2, concat_axis=0, tiled=True)
    count_lev = columns.shape[0]
    upper = lax.axis_index("lat_hi") == 0
    send = jnp.where(upper, columns[count_lev - reach :], columns[:reach])
    recv = lax.ppermute(send, "lat_hi", [(0, 1), (1, 0)])
    zeros = jnp.zeros_like(recv)
    below = jnp.where(upper, zeros, recv)
    above = jnp.where(upper, recv, zeros)
    padded = jnp.concatenate([below, columns, above], axis=0)
    taps = [padded[tap_index : tap_index + count_lev] for tap_index in range(w_vert.shape[0])]
    mixed = lax.all_to_all(
        vertical(taps, w_vert, b_vert), "lat_lo", split_axis=0, concat_axis=2, tiled=True
    )
    masked = mixed * ocean_mask[:, None].astype(jnp.bfloat16)
    extended = jnp.concatenate([halo_masked[..., :reach], masked, halo_masked[..., reach:]], axis=3)
    extended = jnp.pad(extended, ((0, 0), (0, 0), (2, 2), (0, 0)))
    channels, rows_lat, cols_lon = (masked.shape[1], masked.shape[2], masked.shape[3])
    summed = jnp.zeros(masked.shape, jnp.float32)
    for row_tap in range(w_horiz.shape[0]):
        stacked = jnp.concatenate(
            [
                extended[:, :, row_tap : row_tap + rows_lat, col_tap : col_tap + cols_lon]
                for col_tap in range(w_horiz.shape[2])
            ],
            axis=1,
        )
        kernel = w_horiz[row_tap].reshape(channels, -1)
        summed = summed + jnp.einsum(
            "oj,njab->noab", kernel, stacked, preferred_element_type=jnp.float32
        )
    ocean = ocean_mask[:, None].astype(jnp.float32)
    return (fields.astype(jnp.float32) + ocean * (summed + b_horiz[None, :, None, None])).astype(
        jnp.bfloat16
    )


def solution(mesh):
    halves = 2
    lon_count, lat_count = mesh.devices.shape
    split = jax.sharding.Mesh(
        mesh.devices.reshape(lon_count, halves, lat_count // halves), ("lon", "lat_hi", "lat_lo")
    )
    lat = ("lat_hi", "lat_lo")
    placed = (P(lat, None, None, "lon"), P(lat, None, "lon"), P(), P(), P(), P(), P())
    return jax.shard_map(
        local, mesh=split, in_specs=placed, out_specs=P(lat, None, None, "lon"), check_vma=False
    )
```

profile of v0, /device:TPU:1, one launch (start us, length us, event | category | flops | bytes accessed | tf_op | source)
XLA Modules:
  0.0 129.0 jit_solution(12597623093102594426)
XLA Ops:
  0.0 0.9 fusion.130
  0.9 16.2 %collective-permute-start.7 = (s32[1,32,2]{1,2,0:T(2,128)S(1)}, s32[1,32,2]{1,2,0:T(2,128)S(1)}, u32[]{:S(2)}, u32[]{:S(2)}) collective-permute-start(s32[1,32,2]{1,2,0:T(2,128)S(1)} %copy.167), channel_id=1, source_target_pairs={{16,0},{32,16},{48,32},{64,48},{80,64},{96,80},{112,96},{128,112},... | collective-permute-start | bytes 776 | tf_op jit(solution)/shard_map/ppermute | solution.py:54
  17.1 0.1 copy.166
  17.2 1.9 %collective-permute-start.6 = (s32[1,32,2]{1,2,0:T(2,128)S(1)}, s32[1,32,2]{1,2,0:T(2,128)S(1)}, u32[]{:S(2)}, u32[]{:S(2)}) collective-permute-start(s32[1,32,2]{1,2,0:T(2,128)S(1)} %copy.166), channel_id=1, source_target_pairs={{0,16},{16,32},{32,48},{48,64},{64,80},{80,96},{96,112},{112,128},... | collective-permute-start | bytes 776 | tf_op jit(solution)/shard_map/ppermute | solution.py:53
  19.1 1.2 convert_reduce_fusion
  20.3 1.3 fusion.51
  21.7 2.2 %fusion.70 = bf16[1,64,32,128]{3,1,0,2:T(8,128)(2,1)} fusion(f32[64]{0:T(128)} %param.9, f32[32,128]{1,0:T(8,128)S(1)} %add_rsqrt_fusion, f32[32,128]{1,0:T(8,128)S(1)} %broadcast_multiply_fusion, bf16[1,64,32,128]{3,2,1,0:T(8,128)(2,1)} %param.7), kind=kLoop, calls=%fused_computation.71 | loop fusion | flops 1310720 | bytes 1081600 | tf_op jit(solution)/shard_map/convert_element_type | solution.py:24
  23.9 5.3 %all-to-all-start = ((bf16[1,64,32,128]{3,1,0,2:T(8,128)(2,1)}), bf16[1,64,32,128]{3,1,0,2:T(8,128)(2,1)S(1)}, u32[]{:S(2)}, u32[]{:S(2)}) async-start(bf16[1,64,32,128]{3,1,0,2:T(8,128)(2,1)} %fusion.70), calls=%async_computation | async-start | bytes 1048576 | tf_op jit(solution)/shard_map/all_to_all | solution.py:72
  29.1 0.2 fusion.127
  29.4 0.5 copy.160
  29.8 12.4 %collective-permute-start.1 = (bf16[1,64,32,2]{2,1,3,0:T(8,128)(2,1)S(1)}, bf16[1,64,32,2]{2,1,3,0:T(8,128)(2,1)S(1)}, u32[]{:S(2)}, u32[]{:S(2)}) collective-permute-start(bf16[1,64,32,2]{2,1,3,0:T(8,128)(2,1)S(1)} %copy.160), channel_id=1, source_target_pairs={{16,0},{32,16},{48,32},{64,48},{80,64},{96,80},{112,96},{128,112},... | collective-permute-start | bytes 24584 | tf_op jit(solution)/shard_map/ppermute | solution.py:54
  42.2 0.5 copy.159
  42.7 1.9 %collective-permute-start = (bf16[1,64,32,2]{2,1,3,0:T(8,128)(2,1)S(1)}, bf16[1,64,32,2]{2,1,3,0:T(8,128)(2,1)S(1)}, u32[]{:S(2)}, u32[]{:S(2)}) collective-permute-start(bf16[1,64,32,2]{2,1,3,0:T(8,128)(2,1)S(1)} %copy.159), channel_id=1, source_target_pairs={{0,16},{16,32},{32,48},{48,64},{64,80},{80,96},{96,112},{112,128},... | collective-permute-start | bytes 24584 | tf_op jit(solution)/shard_map/ppermute | solution.py:53
  44.6 0.1 mul.183
  44.8 0.1 copy.125
  44.9 0.1 copy.131
  45.0 0.1 copy.127
  45.2 0.1 copy.135
  45.3 0.1 copy.133
  45.5 12.0 %collective-permute-done = bf16[1,64,32,2]{2,1,3,0:T(8,128)(2,1)S(1)} collective-permute-done((bf16[1,64,32,2]{2,1,3,0:T(8,128)(2,1)S(1)}, bf16[1,64,32,2]{2,1,3,0:T(8,128)(2,1)S(1)}, u32[]{:S(2)}, u32[]{:S(2)}) %collective-permute-start) | collective-permute-done | bytes 8224 | tf_op jit(solution)/shard_map/ppermute | solution.py:53
  57.5 0.1 fusion.85
  57.6 1.3 %collective-permute-start.5 = (bf16[1,64,32,4]{2,1,3,0:T(8,128)(2,1)S(1)}, bf16[1,64,32,4]{2,1,3,0:T(8,128)(2,1)S(1)}, u32[]{:S(2)}, u32[]{:S(2)}) collective-permute-start(bf16[1,64,32,4]{2,1,3,0:T(8,128)(2,1)S(1)} %fusion.85), channel_id=1, source_target_pairs={{2,0},{3,1},{4,2},{5,3},{6,4},{7,5},{8,6},{9,7},{10,8},{11,9},{12,... | collective-permute-start | bytes 49160 | tf_op jit(solution)/shard_map/ppermute | solution.py:45
  58.9 3.8 %collective-permute-start.4 = (bf16[1,64,32,4]{2,1,3,0:T(8,128)(2,1)S(1)}, bf16[1,64,32,4]{2,1,3,0:T(8,128)(2,1)S(1)}, u32[]{:S(2)}, u32[]{:S(2)}) collective-permute-start(bf16[1,64,32,4]{2,1,3,0:T(8,128)(2,1)S(1)} %fusion.85), channel_id=1, source_target_pairs={{1,0},{2,1},{3,2},{4,3},{5,4},{6,5},{7,6},{8,7},{9,8},{10,9},{11,1... | collective-permute-start | bytes 49160 | tf_op jit(solution)/shard_map/ppermute | solution.py:45
  62.7 4.2 %collective-permute-start.3 = (bf16[1,64,32,4]{2,1,3,0:T(8,128)(2,1)S(1)}, bf16[1,64,32,4]{2,1,3,0:T(8,128)(2,1)S(1)}, u32[]{:S(2)}, u32[]{:S(2)}) collective-permute-start(bf16[1,64,32,4]{2,1,3,0:T(8,128)(2,1)S(1)} %fusion.85), channel_id=1, source_target_pairs={{0,1},{1,2},{2,3},{3,4},{4,5},{5,6},{6,7},{7,8},{8,9},{9,10},{10,1... | collective-permute-start | bytes 49160 | tf_op jit(solution)/shard_map/ppermute | solution.py:45
  66.9 2.0 %collective-permute-start.2 = (bf16[1,64,32,4]{2,1,3,0:T(8,128)(2,1)S(1)}, bf16[1,64,32,4]{2,1,3,0:T(8,128)(2,1)S(1)}, u32[]{:S(2)}, u32[]{:S(2)}) collective-permute-start(bf16[1,64,32,4]{2,1,3,0:T(8,128)(2,1)S(1)} %fusion.85), channel_id=1, source_target_pairs={{0,2},{1,3},{2,4},{3,5},{4,6},{5,7},{6,8},{7,9},{8,10},{9,11},{10,... | collective-permute-start | bytes 49160 | tf_op jit(solution)/shard_map/ppermute | solution.py:45
  68.9 0.2 fusion.95
  69.2 0.2 fusion.100
  69.4 0.9 collective-permute-done.2
  70.2 0.2 fusion.50
  70.5 26.1 %collective-permute-start.8 = (bf16[2,64,4,128]{3,1,2,0:T(8,128)(2,1)S(1)}, bf16[2,64,4,128]{3,1,2,0:T(8,128)(2,1)S(1)}, u32[]{:S(2)}, u32[]{:S(2)}) collective-permute-start(bf16[2,64,4,128]{3,1,2,0:T(8,128)(2,1)S(1)} %fusion.86), channel_id=1, source_target_pairs={{0,8},{8,0},{1,9},{9,1},{2,10},{10,2},{3,11},{11,3},{4,12},{12,4},... | collective-permute-start | bytes 393224 | tf_op jit(solution)/shard_map/ppermute | solution.py:76
  96.6 0.2 fusion.97
  96.8 3.3 %collective-permute-done.8 = bf16[2,64,4,128]{3,1,2,0:T(8,128)(2,1)S(1)} collective-permute-done((bf16[2,64,4,128]{3,1,2,0:T(8,128)(2,1)S(1)}, bf16[2,64,4,128]{3,1,2,0:T(8,128)(2,1)S(1)}, u32[]{:S(2)}, u32[]{:S(2)}) %collective-permute-start.8) | collective-permute-done | bytes 131104 | tf_op jit(solution)/shard_map/ppermute | solution.py:76
  100.1 0.1 fusion.73
  100.3 0.3 fusion.79
  100.6 0.4 convolution_add_fusion.3
  101.0 0.3 convolution_add_fusion.2
  101.4 0.4 convolution_add_fusion.1
  101.7 0.4 fusion.26
  102.1 1.2 fusion.61
  103.3 4.3 %all-to-all-start.1 = ((bf16[8,64,4,128]{3,1,2,0:T(8,128)(2,1)}), bf16[8,64,4,128]{3,1,2,0:T(8,128)(2,1)S(1)}, u32[]{:S(2)}, u32[]{:S(2)}) async-start(bf16[8,64,4,128]{3,1,2,0:T(8,128)(2,1)} %fusion.61), calls=%async_computation.1 | async-start | bytes 1048576 | tf_op jit(solution)/shard_map/all_to_all | solution.py:82
  107.7 0.2 fusion.49
  107.9 0.1 copy.113
  108.0 0.1 fusion.106
  108.1 0.3 copy.123
  108.4 0.3 copy.124
  108.8 8.4 %all-to-all-done.1 = bf16[8,64,4,128]{3,1,2,0:T(8,128)(2,1)S(1)} async-done(((bf16[8,64,4,128]{3,1,2,0:T(8,128)(2,1)}), bf16[8,64,4,128]{3,1,2,0:T(8,128)(2,1)S(1)}, u32[]{:S(2)}, u32[]{:S(2)}) %all-to-all-start.1) | async-done | bytes 524320 | tf_op jit(solution)/shard_map/all_to_all | solution.py:82
  117.2 0.3 fusion.69
  117.5 0.6 fusion.47
  118.1 0.5 fusion.72
  118.6 0.2 constant_dynamic-update-slice_fusion
  118.8 0.5 fusion.67
  119.3 0.5 fusion.71
  119.9 0.4 slice_dynamic-update-slice_fusion.19
  120.3 0.8 slice_dynamic-update-slice_fusion.18
  121.1 0.9 slice_dynamic-update-slice_fusion.17
  122.0 0.9 slice_dynamic-update-slice_fusion.16
  122.8 0.9 slice_dynamic-update-slice_fusion.15
  123.7 0.3 slice_dynamic-update-slice_fusion
  124.0 0.7 fusion.4
  124.7 0.7 fusion.2
  125.4 0.7 fusion.6
  126.1 0.7 fusion
  126.8 1.0 fusion.41
  127.8 1.1 copy.137
  (38 shorter events, 0.4 us)
Async XLA Ops:
  0.0 29.1 %copy-start = (bf16[1,64,32,128]{3,2,1,0:T(8,128)(2,1)S(1)}, bf16[1,64,32,128]{3,2,1,0:T(8,128)(2,1)}, u32[]{:S(2)}) copy-start(bf16[1,64,32,128]{3,2,1,0:T(8,128)(2,1)} %param.7) | copy-start | bytes 1572868
  0.9 44.5 %collective-permute-start.7 = (s32[1,32,2]{1,2,0:T(2,128)S(1)}, s32[1,32,2]{1,2,0:T(2,128)S(1)}, u32[]{:S(2)}, u32[]{:S(2)}) collective-permute-start(s32[1,32,2]{1,2,0:T(2,128)S(1)} %copy.167), channel_id=1, source_target_pairs={{16,0},{32,16},{48,32},{64,48},{80,64},{96,80},{112,96},{128,112},... | collective-permute-start | bytes 776 | tf_op jit(solution)/shard_map/ppermute | solution.py:54
  17.2 28.3 %collective-permute-start.6 = (s32[1,32,2]{1,2,0:T(2,128)S(1)}, s32[1,32,2]{1,2,0:T(2,128)S(1)}, u32[]{:S(2)}, u32[]{:S(2)}) collective-permute-start(s32[1,32,2]{1,2,0:T(2,128)S(1)} %copy.166), channel_id=1, source_target_pairs={{0,16},{16,32},{32,48},{48,64},{64,80},{80,96},{96,112},{112,128},... | collective-permute-start | bytes 776 | tf_op jit(solution)/shard_map/ppermute | solution.py:53
  21.6 23.0 %copy-start.4 = (f32[64]{0:T(128)S(1)}, f32[64]{0:T(128)}, u32[]{:S(2)}) copy-start(f32[64]{0:T(128)} %param.9) | copy-start | bytes 772
  21.7 23.1 %copy-start.3 = (s32[1,32,128]{2,1,0:T(8,128)S(1)}, s32[1,32,128]{2,1,0:T(8,128)}, u32[]{:S(2)}) copy-start(s32[1,32,128]{2,1,0:T(8,128)} %param.8) | copy-start | bytes 49156
  21.7 23.1 %copy-start.1 = (bf16[5,64,5,64]{3,1,2,0:T(8,128)(2,1)S(1)}, bf16[5,64,5,64]{3,1,2,0:T(8,128)(2,1)}, u32[]{:S(2)}) copy-start(bf16[5,64,5,64]{3,1,2,0:T(8,128)(2,1)} %param.12) | copy-start | bytes 614404
  23.9 46.6 %all-to-all-start = ((bf16[1,64,32,128]{3,1,0,2:T(8,128)(2,1)}), bf16[1,64,32,128]{3,1,0,2:T(8,128)(2,1)S(1)}, u32[]{:S(2)}, u32[]{:S(2)}) async-start(bf16[1,64,32,128]{3,1,0,2:T(8,128)(2,1)} %fusion.70), calls=%async_computation | async-start | bytes 1048576 | tf_op jit(solution)/shard_map/all_to_all | solution.py:72
  29.1 39.8 %copy-start.2 = (bf16[5,8,8,8]{3,2,1,0:T(8,128)(2,1)S(1)}, bf16[5,8,8,8]{3,2,1,0:T(8,128)(2,1)}, u32[]{:S(2)}) copy-start(bf16[5,8,8,8]{3,2,1,0:T(8,128)(2,1)} %param.10) | copy-start | bytes 15364
  29.8 15.6 %collective-permute-start.1 = (bf16[1,64,32,2]{2,1,3,0:T(8,128)(2,1)S(1)}, bf16[1,64,32,2]{2,1,3,0:T(8,128)(2,1)S(1)}, u32[]{:S(2)}, u32[]{:S(2)}) collective-permute-start(bf16[1,64,32,2]{2,1,3,0:T(8,128)(2,1)S(1)} %copy.160), channel_id=1, source_target_pairs={{16,0},{32,16},{48,32},{64,48},{80,64},{96,80},{112,96},{128,112},... | collective-permute-start | bytes 24584 | tf_op jit(solution)/shard_map/ppermute | solution.py:54
  42.7 14.8 %collective-permute-start = (bf16[1,64,32,2]{2,1,3,0:T(8,128)(2,1)S(1)}, bf16[1,64,32,2]{2,1,3,0:T(8,128)(2,1)S(1)}, u32[]{:S(2)}, u32[]{:S(2)}) collective-permute-start(bf16[1,64,32,2]{2,1,3,0:T(8,128)(2,1)S(1)} %copy.159), channel_id=1, source_target_pairs={{0,16},{16,32},{32,48},{48,64},{64,80},{80,96},{96,112},{112,128},... | collective-permute-start | bytes 24584 | tf_op jit(solution)/shard_map/ppermute | solution.py:53
  57.6 39.0 %collective-permute-start.5 = (bf16[1,64,32,4]{2,1,3,0:T(8,128)(2,1)S(1)}, bf16[1,64,32,4]{2,1,3,0:T(8,128)(2,1)S(1)}, u32[]{:S(2)}, u32[]{:S(2)}) collective-permute-start(bf16[1,64,32,4]{2,1,3,0:T(8,128)(2,1)S(1)} %fusion.85), channel_id=1, source_target_pairs={{2,0},{3,1},{4,2},{5,3},{6,4},{7,5},{8,6},{9,7},{10,8},{11,9},{12,... | collective-permute-start | bytes 49160 | tf_op jit(solution)/shard_map/ppermute | solution.py:45
  58.9 48.7 %collective-permute-start.4 = (bf16[1,64,32,4]{2,1,3,0:T(8,128)(2,1)S(1)}, bf16[1,64,32,4]{2,1,3,0:T(8,128)(2,1)S(1)}, u32[]{:S(2)}, u32[]{:S(2)}) collective-permute-start(bf16[1,64,32,4]{2,1,3,0:T(8,128)(2,1)S(1)} %fusion.85), channel_id=1, source_target_pairs={{1,0},{2,1},{3,2},{4,3},{5,4},{6,5},{7,6},{8,7},{9,8},{10,9},{11,1... | collective-permute-start | bytes 49160 | tf_op jit(solution)/shard_map/ppermute | solution.py:45
  62.7 6.5 %collective-permute-start.3 = (bf16[1,64,32,4]{2,1,3,0:T(8,128)(2,1)S(1)}, bf16[1,64,32,4]{2,1,3,0:T(8,128)(2,1)S(1)}, u32[]{:S(2)}, u32[]{:S(2)}) collective-permute-start(bf16[1,64,32,4]{2,1,3,0:T(8,128)(2,1)S(1)} %fusion.85), channel_id=1, source_target_pairs={{0,1},{1,2},{2,3},{3,4},{4,5},{5,6},{6,7},{7,8},{8,9},{9,10},{10,1... | collective-permute-start | bytes 49160 | tf_op jit(solution)/shard_map/ppermute | solution.py:45
  66.9 3.3 %collective-permute-start.2 = (bf16[1,64,32,4]{2,1,3,0:T(8,128)(2,1)S(1)}, bf16[1,64,32,4]{2,1,3,0:T(8,128)(2,1)S(1)}, u32[]{:S(2)}, u32[]{:S(2)}) collective-permute-start(bf16[1,64,32,4]{2,1,3,0:T(8,128)(2,1)S(1)} %fusion.85), channel_id=1, source_target_pairs={{0,2},{1,3},{2,4},{3,5},{4,6},{5,7},{6,8},{7,9},{8,10},{9,11},{10,... | collective-permute-start | bytes 49160 | tf_op jit(solution)/shard_map/ppermute | solution.py:45
  70.5 29.6 %collective-permute-start.8 = (bf16[2,64,4,128]{3,1,2,0:T(8,128)(2,1)S(1)}, bf16[2,64,4,128]{3,1,2,0:T(8,128)(2,1)S(1)}, u32[]{:S(2)}, u32[]{:S(2)}) collective-permute-start(bf16[2,64,4,128]{3,1,2,0:T(8,128)(2,1)S(1)} %fusion.86), channel_id=1, source_target_pairs={{0,8},{8,0},{1,9},{9,1},{2,10},{10,2},{3,11},{11,3},{4,12},{12,4},... | collective-permute-start | bytes 393224 | tf_op jit(solution)/shard_map/ppermute | solution.py:76
  101.4 0.7 copy-start.5
  103.3 13.8 %all-to-all-start.1 = ((bf16[8,64,4,128]{3,1,2,0:T(8,128)(2,1)}), bf16[8,64,4,128]{3,1,2,0:T(8,128)(2,1)S(1)}, u32[]{:S(2)}, u32[]{:S(2)}) async-start(bf16[8,64,4,128]{3,1,2,0:T(8,128)(2,1)} %fusion.61), calls=%async_computation.1 | async-start | bytes 1048576 | tf_op jit(solution)/shard_map/all_to_all | solution.py:82
  126.1 0.7 copy-start.6
where the time goes:
time: 130 us; the launch traced here: 129 us
  starting transfers between devices  79.3 us (61%)
  waiting for transfers between devices  24.5 us (19%)
  other arithmetic  9.11 us (7%)
  local copies, waits for them, and re-layouts  8.99 us (7%)
  matrix products  6.58 us (5%)
    ppermute x2, starting transfers between devices, lon_halo(): after = lax.ppermute(block[..., :width], 'lon', down)  28.5 us
    ppermute x1, starting transfers between devices, local(): recv = lax.ppermute(send, 'lat_hi', [(0, 1), (1, 0)])  26.1 us
    ppermute x2, waiting for transfers between devices, lon_halo(): before = lax.ppermute(block[..., length - width:], 'lon', up)  12 us
    ppermute x4, starting transfers between devices, shifted(): return lax.ppermute(block, axis, pairs)  11.3 us
    all_to_all x1, waiting for transfers between devices, local(): lax.all_to_all(vertical(taps, w_vert, b_vert), 'lat_lo', split_axis=0, co...  8.39 us
    all_to_all x1, starting transfers between devices, local(): lax.all_to_all(normed, 'lat_lo', split_axis=2, concat_axis=0, tiled=True)  5.25 us
    all_to_all x1, starting transfers between devices, local(): lax.all_to_all(vertical(taps, w_vert, b_vert), 'lat_lo', split_axis=0, co...  4.31 us
    unnamed x22, local copies, waits for them, and re-layouts  4.11 us
  transfers between devices with their start and end apart: 11, of which 4 were waited for; matrix products, arithmetic and copies ran while one was open for 9% of the time, Pallas kernels for 0%

commit v1 on v0

--- a/solution.py
+++ b/solution.py
@@ -69,7 +69,12 @@
     halo_mask = jnp.concatenate([mask_before, mask_after], axis=2)
     halo_masked = vertical(halo_taps, w_vert, b_vert) * halo_mask[:, None].astype(jnp.bfloat16)
     normed = normalize(fields, norm_gain)
-    columns = lax.all_to_all(normed, "lat_lo", split_axis=2, concat_axis=0, tiled=True)
+    columns = jnp.concatenate(
+        lax.all_to_all(
+            jnp.stack(jnp.split(normed, lax.axis_size("lat_lo"), axis=2)), "lat_lo", 0, 0
+        ),
+        axis=0,
+    )
     count_lev = columns.shape[0]
     upper = lax.axis_index("lat_hi") == 0
     send = jnp.where(upper, columns[count_lev - reach :], columns[:reach])

time: 130 us -> 134 us (1.031)
  local copies, waits for them, and re-layouts: 8.99 us -> 14.1 us
    unnamed x22 -> x29, local copies, waits for them, and re-layouts: 4.11 us -> 8.54 us
  transfers between devices with their start and end apart: 11 -> 11, of which waited for: 4 -> 4; matrix products, arithmetic and copies ran while one was open for 9% -> 12% of each run, Pallas kernels for 0% -> 0%
where the time goes in v1:
time: 134 us; the launch traced here: 133 us
  starting transfers between devices  79.3 us (59%)
  waiting for transfers between devices  24.5 us (18%)
  local copies, waits for them, and re-layouts  14.1 us (11%)
  other arithmetic  8.26 us (6%)
  matrix products  6.58 us (5%)
    ppermute x2, starting transfers between devices, lon_halo(): after = lax.ppermute(block[..., :width], 'lon', down)  28.5 us
    ppermute x1, starting transfers between devices, local(): recv = lax.ppermute(send, 'lat_hi', [(0, 1), (1, 0)])  26.1 us
    ppermute x2, waiting for transfers between devices, lon_halo(): before = lax.ppermute(block[..., length - width:], 'lon', up)  12 us
    ppermute x4, starting transfers between devices, shifted(): return lax.ppermute(block, axis, pairs)  11.3 us
    unnamed x29, local copies, waits for them, and re-layouts  8.54 us
    all_to_all x1, waiting for transfers between devices, local(): lax.all_to_all(vertical(taps, w_vert, b_vert), 'lat_lo', split_axis=0, co...  8.39 us
    all_to_all x1, starting transfers between devices, local(): lax.all_to_all(jnp.stack(jnp.split(normed, lax.axis_size('lat_lo'), axis=...  5.25 us
    all_to_all x1, starting transfers between devices, local(): lax.all_to_all(vertical(taps, w_vert, b_vert), 'lat_lo', split_axis=0, co...  4.31 us
  transfers between devices with their start and end apart: 11, of which 4 were waited for; matrix products, arithmetic and copies ran while one was open for 12% of the time, Pallas kernels for 0%

profile of v1, /device:TPU:1, one launch (start us, length us, event | category | flops | bytes accessed | tf_op | source)
XLA Modules:
  0.0 133.2 jit_solution(7585489422161689558)
XLA Ops:
  0.0 0.9 fusion.129
  0.9 16.2 %collective-permute-start.7 = (s32[1,32,2]{1,2,0:T(2,128)S(1)}, s32[1,32,2]{1,2,0:T(2,128)S(1)}, u32[]{:S(2)}, u32[]{:S(2)}) collective-permute-start(s32[1,32,2]{1,2,0:T(2,128)S(1)} %copy.173), channel_id=1, source_target_pairs={{16,0},{32,16},{48,32},{64,48},{80,64},{96,80},{112,96},{128,112},... | collective-permute-start | bytes 776 | tf_op jit(solution)/shard_map/ppermute | solution.py:54
  17.2 1.9 %collective-permute-start.6 = (s32[1,32,2]{1,2,0:T(2,128)S(1)}, s32[1,32,2]{1,2,0:T(2,128)S(1)}, u32[]{:S(2)}, u32[]{:S(2)}) collective-permute-start(s32[1,32,2]{1,2,0:T(2,128)S(1)} %copy.172), channel_id=1, source_target_pairs={{0,16},{16,32},{32,48},{48,64},{64,80},{80,96},{96,112},{112,128},... | collective-permute-start | bytes 776 | tf_op jit(solution)/shard_map/ppermute | solution.py:53
  19.1 1.2 convert_reduce_fusion
  20.3 1.3 fusion.51
  21.6 1.4 %fusion.53 = bf16[1,64,32,128]{3,1,2,0:T(8,128)(2,1)S(1)} fusion(f32[64]{0:T(128)} %param.9, f32[32,128]{1,0:T(8,128)S(1)} %add_rsqrt_fusion, f32[32,128]{1,0:T(8,128)S(1)} %broadcast_multiply_fusion, bf16[1,64,32,128]{3,2,1,0:T(8,128)(2,1)} %param.7), kind=kLoop, calls=%fused_computation.45 | loop fusion | flops 1310720 | bytes 1081600 | tf_op jit(solution)/shard_map/convert_element_type | solution.py:24
  23.0 0.6 constant_dynamic-update-slice_fusion.7
  23.6 0.6 constant_dynamic-update-slice_fusion.6
  24.3 0.6 constant_dynamic-update-slice_fusion.5
  24.9 0.6 constant_dynamic-update-slice_fusion.4
  25.5 0.6 constant_dynamic-update-slice_fusion.3
  26.2 0.6 constant_dynamic-update-slice_fusion.2
  26.8 0.6 constant_dynamic-update-slice_fusion.1
  27.4 0.6 constant_dynamic-update-slice_fusion
  28.1 5.3 %all-to-all-start = ((bf16[8,1,64,4,128]{4,2,3,1,0:T(8,128)(2,1)}), bf16[8,1,64,4,128]{4,2,3,1,0:T(8,128)(2,1)S(1)}, u32[]{:S(2)}, u32[]{:S(2)}) async-start(bf16[8,1,64,4,128]{4,2,3,1,0:T(8,128)(2,1)} %constant_dynamic-update-slice_fusion), calls=%async_computation | async-start | bytes 1048576 | tf_op jit(solution)/shard_map/all_to_all | solution.py:73
  33.3 0.2 fusion.126
  33.6 0.5 copy.166
  34.0 12.4 %collective-permute-start.1 = (bf16[1,64,32,2]{2,1,3,0:T(8,128)(2,1)S(1)}, bf16[1,64,32,2]{2,1,3,0:T(8,128)(2,1)S(1)}, u32[]{:S(2)}, u32[]{:S(2)}) collective-permute-start(bf16[1,64,32,2]{2,1,3,0:T(8,128)(2,1)S(1)} %copy.166), channel_id=1, source_target_pairs={{16,0},{32,16},{48,32},{64,48},{80,64},{96,80},{112,96},{128,112},... | collective-permute-start | bytes 24584 | tf_op jit(solution)/shard_map/ppermute | solution.py:54
  46.4 0.5 copy.165
  46.9 1.9 %collective-permute-start = (bf16[1,64,32,2]{2,1,3,0:T(8,128)(2,1)S(1)}, bf16[1,64,32,2]{2,1,3,0:T(8,128)(2,1)S(1)}, u32[]{:S(2)}, u32[]{:S(2)}) collective-permute-start(bf16[1,64,32,2]{2,1,3,0:T(8,128)(2,1)S(1)} %copy.165), channel_id=1, source_target_pairs={{0,16},{16,32},{32,48},{48,64},{64,80},{80,96},{96,112},{112,128},... | collective-permute-start | bytes 24584 | tf_op jit(solution)/shard_map/ppermute | solution.py:53
  49.1 0.1 copy.137
  49.2 0.1 copy.133
  49.7 12.0 %collective-permute-done = bf16[1,64,32,2]{2,1,3,0:T(8,128)(2,1)S(1)} collective-permute-done((bf16[1,64,32,2]{2,1,3,0:T(8,128)(2,1)S(1)}, bf16[1,64,32,2]{2,1,3,0:T(8,128)(2,1)S(1)}, u32[]{:S(2)}, u32[]{:S(2)}) %collective-permute-start) | collective-permute-done | bytes 8224 | tf_op jit(solution)/shard_map/ppermute | solution.py:53
  61.8 1.3 collective-permute-start.5
  63.1 3.8 %collective-permute-start.4 = (bf16[1,64,32,4]{2,1,3,0:T(8,128)(2,1)S(1)}, bf16[1,64,32,4]{2,1,3,0:T(8,128)(2,1)S(1)}, u32[]{:S(2)}, u32[]{:S(2)}) collective-permute-start(bf16[1,64,32,4]{2,1,3,0:T(8,128)(2,1)S(1)} %fusion.84), channel_id=1, source_target_pairs={{1,0},{2,1},{3,2},{4,3},{5,4},{6,5},{7,6},{8,7},{9,8},{10,9},{11,1... | collective-permute-start | bytes 49160 | tf_op jit(solution)/shard_map/ppermute | solution.py:45
  66.9 4.2 %collective-permute-start.3 = (bf16[1,64,32,4]{2,1,3,0:T(8,128)(2,1)S(1)}, bf16[1,64,32,4]{2,1,3,0:T(8,128)(2,1)S(1)}, u32[]{:S(2)}, u32[]{:S(2)}) collective-permute-start(bf16[1,64,32,4]{2,1,3,0:T(8,128)(2,1)S(1)} %fusion.84), channel_id=1, source_target_pairs={{0,1},{1,2},{2,3},{3,4},{4,5},{5,6},{6,7},{7,8},{8,9},{9,10},{10,1... | collective-permute-start | bytes 49160 | tf_op jit(solution)/shard_map/ppermute | solution.py:45
  71.1 2.0 %collective-permute-start.2 = (bf16[1,64,32,4]{2,1,3,0:T(8,128)(2,1)S(1)}, bf16[1,64,32,4]{2,1,3,0:T(8,128)(2,1)S(1)}, u32[]{:S(2)}, u32[]{:S(2)}) collective-permute-start(bf16[1,64,32,4]{2,1,3,0:T(8,128)(2,1)S(1)} %fusion.84), channel_id=1, source_target_pairs={{0,2},{1,3},{2,4},{3,5},{4,6},{5,7},{6,8},{7,9},{8,10},{9,11},{10,... | collective-permute-start | bytes 49160 | tf_op jit(solution)/shard_map/ppermute | solution.py:45
  73.1 0.2 fusion.94
  73.4 0.2 fusion.99
  73.6 0.9 collective-permute-done.2
  74.4 0.2 fusion.50
  74.7 26.1 %collective-permute-start.8 = (bf16[2,64,4,128]{3,1,2,0:T(8,128)(2,1)S(1)}, bf16[2,64,4,128]{3,1,2,0:T(8,128)(2,1)S(1)}, u32[]{:S(2)}, u32[]{:S(2)}) collective-permute-start(bf16[2,64,4,128]{3,1,2,0:T(8,128)(2,1)S(1)} %fusion.85), channel_id=1, source_target_pairs={{0,8},{8,0},{1,9},{9,1},{2,10},{10,2},{3,11},{11,3},{4,12},{12,4},... | collective-permute-start | bytes 393224 | tf_op jit(solution)/shard_map/ppermute | solution.py:81
  100.8 0.2 fusion.96
  101.0 3.3 %collective-permute-done.8 = bf16[2,64,4,128]{3,1,2,0:T(8,128)(2,1)S(1)} collective-permute-done((bf16[2,64,4,128]{3,1,2,0:T(8,128)(2,1)S(1)}, bf16[2,64,4,128]{3,1,2,0:T(8,128)(2,1)S(1)}, u32[]{:S(2)}, u32[]{:S(2)}) %collective-permute-start.8) | collective-permute-done | bytes 131104 | tf_op jit(solution)/shard_map/ppermute | solution.py:81
  104.3 0.1 fusion.72
  104.5 0.3 fusion.78
  104.8 0.3 convolution_add_fusion.3
  105.2 0.3 convolution_add_fusion.2
  105.6 0.4 convolution_add_fusion.1
  105.9 0.4 fusion.26
  106.3 1.2 fusion.61
  107.5 4.3 %all-to-all-start.1 = ((bf16[8,64,4,128]{3,1,2,0:T(8,128)(2,1)}), bf16[8,64,4,128]{3,1,2,0:T(8,128)(2,1)S(1)}, u32[]{:S(2)}, u32[]{:S(2)}) async-start(bf16[8,64,4,128]{3,1,2,0:T(8,128)(2,1)} %fusion.61), calls=%async_computation.1 | async-start | bytes 1048576 | tf_op jit(solution)/shard_map/all_to_all | solution.py:87
  111.9 0.2 fusion.49
  112.3 0.3 copy.129
  112.6 0.3 copy.130
  113.0 8.4 %all-to-all-done.1 = bf16[8,64,4,128]{3,1,2,0:T(8,128)(2,1)S(1)} async-done(((bf16[8,64,4,128]{3,1,2,0:T(8,128)(2,1)}), bf16[8,64,4,128]{3,1,2,0:T(8,128)(2,1)S(1)}, u32[]{:S(2)}, u32[]{:S(2)}) %all-to-all-start.1) | async-done | bytes 524320 | tf_op jit(solution)/shard_map/all_to_all | solution.py:87
  121.4 0.3 fusion.69
  121.7 0.6 fusion.47
  122.3 0.5 fusion.71
  122.8 0.2 constant_dynamic-update-slice_fusion.8
  123.0 0.5 fusion.67
  123.6 0.5 fusion.70
  124.1 0.4 slice_dynamic-update-slice_fusion.19
  124.5 0.8 slice_dynamic-update-slice_fusion.18
  125.3 0.9 slice_dynamic-update-slice_fusion.17
  126.2 0.9 slice_dynamic-update-slice_fusion.16
  127.0 0.9 slice_dynamic-update-slice_fusion.15
  127.9 0.3 slice_dynamic-update-slice_fusion
  128.2 0.7 fusion.4
  128.9 0.7 fusion.2
  129.6 0.7 fusion.6
  130.3 0.7 fusion
  131.0 1.0 fusion.41
  132.0 1.1 copy.143
  (46 shorter events, 1.2 us)
Async XLA Ops:
  0.0 33.3 %copy-start = (bf16[1,64,32,128]{3,2,1,0:T(8,128)(2,1)S(1)}, bf16[1,64,32,128]{3,2,1,0:T(8,128)(2,1)}, u32[]{:S(2)}) copy-start(bf16[1,64,32,128]{3,2,1,0:T(8,128)(2,1)} %param.7) | copy-start | bytes 1572868
  0.9 48.7 %collective-permute-start.7 = (s32[1,32,2]{1,2,0:T(2,128)S(1)}, s32[1,32,2]{1,2,0:T(2,128)S(1)}, u32[]{:S(2)}, u32[]{:S(2)}) collective-permute-start(s32[1,32,2]{1,2,0:T(2,128)S(1)} %copy.173), channel_id=1, source_target_pairs={{16,0},{32,16},{48,32},{64,48},{80,64},{96,80},{112,96},{128,112},... | collective-permute-start | bytes 776 | tf_op jit(solution)/shard_map/ppermute | solution.py:54
  17.2 32.5 %collective-permute-start.6 = (s32[1,32,2]{1,2,0:T(2,128)S(1)}, s32[1,32,2]{1,2,0:T(2,128)S(1)}, u32[]{:S(2)}, u32[]{:S(2)}) collective-permute-start(s32[1,32,2]{1,2,0:T(2,128)S(1)} %copy.172), channel_id=1, source_target_pairs={{0,16},{16,32},{32,48},{48,64},{64,80},{80,96},{96,112},{112,128},... | collective-permute-start | bytes 776 | tf_op jit(solution)/shard_map/ppermute | solution.py:53
  23.6 25.2 %copy-start.4 = (f32[64]{0:T(128)S(1)}, f32[64]{0:T(128)}, u32[]{:S(2)}) copy-start(f32[64]{0:T(128)} %param.9) | copy-start | bytes 772
  23.6 25.3 %copy-start.3 = (s32[1,32,128]{2,1,0:T(8,128)S(1)}, s32[1,32,128]{2,1,0:T(8,128)}, u32[]{:S(2)}) copy-start(s32[1,32,128]{2,1,0:T(8,128)} %param.8) | copy-start | bytes 49156
  23.6 25.3 %copy-start.1 = (bf16[5,64,5,64]{3,1,2,0:T(8,128)(2,1)S(1)}, bf16[5,64,5,64]{3,1,2,0:T(8,128)(2,1)}, u32[]{:S(2)}) copy-start(bf16[5,64,5,64]{3,1,2,0:T(8,128)(2,1)} %param.12) | copy-start | bytes 614404
  28.1 46.6 %all-to-all-start = ((bf16[8,1,64,4,128]{4,2,3,1,0:T(8,128)(2,1)}), bf16[8,1,64,4,128]{4,2,3,1,0:T(8,128)(2,1)S(1)}, u32[]{:S(2)}, u32[]{:S(2)}) async-start(bf16[8,1,64,4,128]{4,2,3,1,0:T(8,128)(2,1)} %constant_dynamic-update-slice_fusion), calls=%async_computation | async-start | bytes 1048576 | tf_op jit(solution)/shard_map/all_to_all | solution.py:73
  33.3 39.8 %copy-start.2 = (bf16[5,8,8,8]{3,2,1,0:T(8,128)(2,1)S(1)}, bf16[5,8,8,8]{3,2,1,0:T(8,128)(2,1)}, u32[]{:S(2)}) copy-start(bf16[5,8,8,8]{3,2,1,0:T(8,128)(2,1)} %param.10) | copy-start | bytes 15364
  34.0 15.6 %collective-permute-start.1 = (bf16[1,64,32,2]{2,1,3,0:T(8,128)(2,1)S(1)}, bf16[1,64,32,2]{2,1,3,0:T(8,128)(2,1)S(1)}, u32[]{:S(2)}, u32[]{:S(2)}) collective-permute-start(bf16[1,64,32,2]{2,1,3,0:T(8,128)(2,1)S(1)} %copy.166), channel_id=1, source_target_pairs={{16,0},{32,16},{48,32},{64,48},{80,64},{96,80},{112,96},{128,112},... | collective-permute-start | bytes 24584 | tf_op jit(solution)/shard_map/ppermute | solution.py:54
  46.9 14.8 %collective-permute-start = (bf16[1,64,32,2]{2,1,3,0:T(8,128)(2,1)S(1)}, bf16[1,64,32,2]{2,1,3,0:T(8,128)(2,1)S(1)}, u32[]{:S(2)}, u32[]{:S(2)}) collective-permute-start(bf16[1,64,32,2]{2,1,3,0:T(8,128)(2,1)S(1)} %copy.165), channel_id=1, source_target_pairs={{0,16},{16,32},{32,48},{48,64},{64,80},{80,96},{96,112},{112,128},... | collective-permute-start | bytes 24584 | tf_op jit(solution)/shard_map/ppermute | solution.py:53
  61.8 39.0 %collective-permute-start.5 = (bf16[1,64,32,4]{2,1,3,0:T(8,128)(2,1)S(1)}, bf16[1,64,32,4]{2,1,3,0:T(8,128)(2,1)S(1)}, u32[]{:S(2)}, u32[]{:S(2)}) collective-permute-start(bf16[1,64,32,4]{2,1,3,0:T(8,128)(2,1)S(1)} %fusion.84), channel_id=1, source_target_pairs={{2,0},{3,1},{4,2},{5,3},{6,4},{7,5},{8,6},{9,7},{10,8},{11,9},{12,... | collective-permute-start | bytes 49160 | tf_op jit(solution)/shard_map/ppermute | solution.py:45
  63.1 48.7 %collective-permute-start.4 = (bf16[1,64,32,4]{2,1,3,0:T(8,128)(2,1)S(1)}, bf16[1,64,32,4]{2,1,3,0:T(8,128)(2,1)S(1)}, u32[]{:S(2)}, u32[]{:S(2)}) collective-permute-start(bf16[1,64,32,4]{2,1,3,0:T(8,128)(2,1)S(1)} %fusion.84), channel_id=1, source_target_pairs={{1,0},{2,1},{3,2},{4,3},{5,4},{6,5},{7,6},{8,7},{9,8},{10,9},{11,1... | collective-permute-start | bytes 49160 | tf_op jit(solution)/shard_map/ppermute | solution.py:45
  66.9 6.5 %collective-permute-start.3 = (bf16[1,64,32,4]{2,1,3,0:T(8,128)(2,1)S(1)}, bf16[1,64,32,4]{2,1,3,0:T(8,128)(2,1)S(1)}, u32[]{:S(2)}, u32[]{:S(2)}) collective-permute-start(bf16[1,64,32,4]{2,1,3,0:T(8,128)(2,1)S(1)} %fusion.84), channel_id=1, source_target_pairs={{0,1},{1,2},{2,3},{3,4},{4,5},{5,6},{6,7},{7,8},{8,9},{9,10},{10,1... | collective-permute-start | bytes 49160 | tf_op jit(solution)/shard_map/ppermute | solution.py:45
  71.1 3.3 %collective-permute-start.2 = (bf16[1,64,32,4]{2,1,3,0:T(8,128)(2,1)S(1)}, bf16[1,64,32,4]{2,1,3,0:T(8,128)(2,1)S(1)}, u32[]{:S(2)}, u32[]{:S(2)}) collective-permute-start(bf16[1,64,32,4]{2,1,3,0:T(8,128)(2,1)S(1)} %fusion.84), channel_id=1, source_target_pairs={{0,2},{1,3},{2,4},{3,5},{4,6},{5,7},{6,8},{7,9},{8,10},{9,11},{10,... | collective-permute-start | bytes 49160 | tf_op jit(solution)/shard_map/ppermute | solution.py:45
  74.7 29.6 %collective-permute-start.8 = (bf16[2,64,4,128]{3,1,2,0:T(8,128)(2,1)S(1)}, bf16[2,64,4,128]{3,1,2,0:T(8,128)(2,1)S(1)}, u32[]{:S(2)}, u32[]{:S(2)}) collective-permute-start(bf16[2,64,4,128]{3,1,2,0:T(8,128)(2,1)S(1)} %fusion.85), channel_id=1, source_target_pairs={{0,8},{8,0},{1,9},{9,1},{2,10},{10,2},{3,11},{11,3},{4,12},{12,4},... | collective-permute-start | bytes 393224 | tf_op jit(solution)/shard_map/ppermute | solution.py:81
  105.6 0.7 copy-start.5
  107.5 13.8 %all-to-all-start.1 = ((bf16[8,64,4,128]{3,1,2,0:T(8,128)(2,1)}), bf16[8,64,4,128]{3,1,2,0:T(8,128)(2,1)S(1)}, u32[]{:S(2)}, u32[]{:S(2)}) async-start(bf16[8,64,4,128]{3,1,2,0:T(8,128)(2,1)} %fusion.61), calls=%async_computation.1 | async-start | bytes 1048576 | tf_op jit(solution)/shard_map/all_to_all | solution.py:87
  130.3 0.7 copy-start.6
